TPU v7x, 32 devices: a whole 2x2x4 slice. The times are simulated.
32 devices in a mesh: seq: 4 (over y, x), res: 8 (over z, core).
Axes of the slice: x: 2, y: 2, z: 4, core: 2. Of those that a mesh axis runs over, the one named last changes fastest.
Arguments:
- alignment: float32 [256, 64, 256], P('seq', 'res'), may hold values from -100 to 100
- pair_features: float32 [64, 64, 128], P('seq', 'res'), may hold values from -100 to 100
- outer_gain: float32 [256], replicated, may hold values from 0.5 to 1.5
- w_outer_in: float32 [256, 64], replicated, may hold values from -0.375 to 0.375
- w_outer_out: float32 [1024, 128], replicated, may hold values from -0.1875 to 0.1875
- pair_gain: float32 [128], replicated, may hold values from 0.5 to 1.5
- w_bias: float32 [128, 8], replicated, may hold values from -30 to 30
- row_gain: float32 [256], replicated, may hold values from 0.5 to 1.5
- w_project: float32 [256, 1024], replicated, may hold values from -0.375 to 0.375
- w_output: float32 [256, 256], replicated, may hold values from -0.375 to 0.375
Outputs:
- alignment_out: float32 [256, 64, 256], P('seq', 'res')
- updated_pair_array: float32 [64, 64, 128], P('seq', 'res')
All inputs are finite; a program needn't handle non-finite values.
Results may differ from a plain program's by a relative error of at most 0.00018.
Values sent between devices are 32-bit elements; how exact they have to be, the bound alone decides.
A program may use at most 128 MiB of HBM per device.

v0:
```python
import jax
import jax.numpy as jnp
from jax import lax
from jax.sharding import PartitionSpec as P

precise = lax.Precision.HIGHEST


def layer_norm(values, scales):
    average = jnp.mean(values, axis=-1, keepdims=True)
    centered = values - average
    variance = jnp.mean(centered * centered, axis=-1, keepdims=True)
    return centered * lax.rsqrt(variance + 1e-05) * scales


def row_attention(sequence, bias_all, row_gain, w_project, w_output):
    residues, channels = sequence.shape
    head_count = bias_all.shape[0]
    head_size = channels // head_count
    normed_rows = layer_norm(sequence, row_gain)
    projected = jnp.dot(
        normed_rows, w_project, precision=precise, preferred_element_type=jnp.float32
    )
    query_map = projected[:, :channels].reshape(residues, head_count, head_size) * head_size ** (
        -0.5
    )
    key_map = projected[:, channels : 2 * channels].reshape(residues, head_count, head_size)
    value_map = projected[:, 2 * channels : 3 * channels].reshape(residues, head_count, head_size)
    gate_map = projected[:, 3 * channels :]
    scores = jnp.einsum("ihd,jhd->hij", query_map, key_map, precision=precise) + bias_all
    weights = jax.nn.softmax(scores, axis=-1)
    mixed_heads = jnp.einsum("hij,jhd->ihd", weights, value_map, precision=precise).reshape(
        residues, channels
    )
    gated_out = jax.nn.sigmoid(gate_map) * mixed_heads
    return sequence + jnp.dot(
        gated_out, w_output, precision=precise, preferred_element_type=jnp.float32
    )


def on_device(
    alignment,
    pair_features,
    outer_gain,
    w_outer_in,
    w_outer_out,
    pair_gain,
    w_bias,
    row_gain,
    w_project,
    w_output,
):
    sequence_local_count, residue_local_count, alignment_channel_count = alignment.shape
    row_block = pair_features.shape[0]
    sequence_group_list = lax.axis_size("res")
    seq_groups = lax.axis_size("seq")
    seq_total = sequence_local_count * seq_groups
    channels = w_outer_in.shape[1] // 2
    normed_rows = layer_norm(alignment, outer_gain)
    both_maps = jnp.einsum("src,cd->sdr", normed_rows, w_outer_in, precision=precise)
    left_maps = both_maps[:, :channels]
    right_maps = both_maps[:, channels:]
    left_all = lax.all_gather(left_maps, "res", axis=2, tiled=True)
    left_rows = lax.all_to_all(left_all, "seq", split_axis=2, concat_axis=0, tiled=True)
    product = jnp.einsum(
        "sxi,syj->ijxy",
        left_rows,
        lax.all_gather(right_maps, "seq", axis=0, tiled=True),
        precision=precise,
    )
    summed = product.reshape(row_block, residue_local_count, channels * channels)
    pair_update = jnp.einsum("ijk,kc->ijc", summed / seq_total, w_outer_out, precision=precise)
    updated_pair_array = pair_features + pair_update
    bias_tile = jnp.einsum(
        "ijc,ch->hij", layer_norm(updated_pair_array, pair_gain), w_bias, precision=precise
    )
    bias_rows = lax.all_gather(bias_tile, "res", axis=2, tiled=True)
    bias_all = lax.all_gather(bias_rows, "seq", axis=1, tiled=True)
    sequence_grouped_rows = alignment.reshape(
        sequence_group_list,
        sequence_local_count // sequence_group_list,
        residue_local_count,
        alignment_channel_count,
    )
    sequences = lax.all_to_all(
        sequence_grouped_rows, "res", split_axis=0, concat_axis=2, tiled=True
    )[0]
    updated = jax.vmap(row_attention, in_axes=(0, None, None, None, None))(
        sequences, bias_all, row_gain, w_project, w_output
    )
    attended = updated[None]
    returned_result = lax.all_to_all(attended, "res", split_axis=2, concat_axis=0, tiled=True)
    return (
        returned_result.reshape(sequence_local_count, residue_local_count, alignment_channel_count),
        updated_pair_array,
    )


def solution(mesh):
    in_specs = (
        P("seq", "res", None),
        P("seq", "res", None),
        P(),
        P(),
        P(),
        P(),
        P(),
        P(),
        P(),
        P(),
    )
    out_specs = (P("seq", "res", None), P("seq", "res", None))
    return jax.shard_map(
        on_device, mesh=mesh, in_specs=in_specs, out_specs=out_specs, check_vma=False
    )
```

profile of v0, /device:TPU:0, one launch (start us, length us, event | category | flops | bytes accessed | tf_op | source)
XLA Modules:
  0.0 148.9 jit_solution(3641051938862273192)
XLA Ops:
  0.6 0.0 copy-start
  0.6 1.3 reduce_sum.65
  1.9 1.3 multiply_reduce_fusion
  3.2 1.7 %convolution_bitcast_fusion = f32[64,64,8]{1,2,0:T(8,128)S(1)} fusion(f32[64,8,256]{2,1,0:T(8,128)} %param.10, f32[256]{0:T(256)} %param.12, f32[64,8]{1,0:T(8,128)S(1)} %add_rsqrt_fusion, f32[64,8]{1,0:T(8,128)S(1)} %broadcast_multiply_fusion, f32[256,64]{0,1:T(8,128)} %param.13), kind=kOutput, calls=%fused_computation.8 | convolution fusion | flops 101056512 | bytes 726016 | tf_op jit(solution)/shard_map/src,cd->sdr/dot_general | solution.py:60
  4.9 0.1 fusion.40
  5.1 25.1 %all_gather.13 = f32[64,32,64]{1,2,0:T(8,128)S(1)} all-gather(f32[64,32,8]{1,2,0:T(8,128)S(1)} %get-tuple-element.5), channel_id=1, replica_groups=mesh['seq'=4,'res'=8] {'res'}, dimensions={2}, use_global_device_ids=true | all-gather | bytes 589824 | tf_op jit(solution)/shard_map/all_gather | solution.py:63
  30.2 2.1 %copy.39 = f32[64,32,64]{0,1,2:T(8,128)} copy(f32[64,32,64]{1,2,0:T(8,128)S(1)} %all_gather.13) | data formatting | bytes 1048576 | tf_op jit(solution)/shard_map/all_gather | solution.py:63
  32.3 2.7 %reshape.99 = f32[4,1,32768]{2,1,0:T(1,128)} reshape(f32[64,32,64]{2,1,0:T(8,128)} %bitcast.73) | data formatting | bytes 1048576
  35.0 3.7 %all-to-all-start.1 = ((f32[4,1,32768]{2,1,0:T(1,128)}), f32[4,1,32768]{2,1,0:T(1,128)S(1)}, u32[]{:S(2)}, u32[]{:S(2)}) async-start(f32[4,1,32768]{2,1,0:T(1,128)} %reshape.99), calls=%async_computation.1 | async-start | bytes 1048576 | tf_op jit(solution)/shard_map/all_to_all | solution.py:64
  38.7 18.5 %all_gather.12 = f32[256,32,8]{1,2,0:T(8,128)S(1)} all-gather(f32[64,32,8]{1,2,0:T(8,128)S(1)} %get-tuple-element.6), channel_id=1, replica_groups=mesh['seq'=4,'res'=8] {'seq'}, dimensions={0}, use_global_device_ids=true | all-gather | bytes 327680 | tf_op jit(solution)/shard_map/all_gather | solution.py:68
  57.2 0.4 copy.49
  57.6 0.0 all-to-all-done.1
  57.6 4.3 %all-to-all-start = ((f32[8,8,8,256]{3,2,1,0:T(8,128)}), f32[8,8,8,256]{3,2,1,0:T(8,128)}, u32[]{:S(2)}, u32[]{:S(2)}) async-start(f32[8,8,8,256]{3,2,1,0:T(8,128)} %bitcast), calls=%async_computation | async-start | bytes 1048576 | tf_op jit(solution)/shard_map/all_to_all | solution.py:85
  62.0 0.5 broadcast.97
  62.5 2.1 %reduce.2 = f32[4,32768]{1,0:T(4,128)S(1)} reduce(f32[4,1,32768]{2,1,0:T(1,128)S(1)} %all-to-all-done.1, f32[]{:T(128)} %broadcast.97), dimensions={1}, to_apply=%all_to_all.38.reduce_sub_computation | reduce | bytes 1048580 | tf_op jit(solution)/shard_map/all_to_all | solution.py:64
  64.6 0.5 reshape.100
  65.2 0.7 copy.59
  65.9 0.6 reshape.94
  66.5 3.2 %multiply_bitcast_fusion = f32[16,8,32,32]{2,1,0,3:T(8,128)} fusion(f32[256,32,8,1]{0,2,3,1:T(8,128)S(1)} %copy.49, f32[256,32,16,1]{0,1,2,3:T(8,128)S(1)} %reshape.94), kind=kOutput, calls=%fused_computation.3 | convolution fusion | flops 402784256 | bytes 1310720 | tf_op jit(solution)/shard_map/sxi,syj->ijxy/dot_general | solution.py:65
  69.7 2.3 %copy.42 = f32[16,8,32,32]{3,2,1,0:T(8,128)S(1)} copy(f32[16,8,32,32]{2,1,0,3:T(8,128)} %multiply_bitcast_fusion) | data formatting | bytes 1048576 | tf_op jit(solution)/shard_map/div | solution.py:72
  71.9 0.0 copy-start.3
  71.9 0.0 copy-start.5
  71.9 0.0 copy-start.6
  72.0 1.7 %div.50 = f32[16,8,1024]{2,1,0:T(8,128)} reshape(f32[16,8,32,32]{3,2,1,0:T(8,128)S(1)} %copy.42) | data formatting | bytes 1048576 | tf_op jit(solution)/shard_map/div | solution.py:72
  73.7 0.0 copy-done.3
  73.7 1.9 %fusion.41 = (f32[16,8]{1,0:T(8,128)S(1)}, f32[16,8,128]{2,1,0:T(8,128)S(1)}) fusion(f32[16,8,128]{2,1,0:T(8,128)S(1)} %copy-done.3, f32[16,8,1024]{2,1,0:T(8,128)} %div.50, f32[1024,128]{1,0:T(8,128)} %param.14), kind=kOutput, calls=%fused_computation.60 | convolution fusion | flops 201359232 | bytes 1180160 | tf_op jit(solution)/shard_map/ijk,kc->ijc/dot_general | solution.py:72
  75.6 0.0 copy-start.2
  75.6 0.0 copy-start.4
  75.7 0.2 multiply_reduce_fusion.2
  75.8 0.0 copy-done.5
  75.8 0.0 copy-done.6
  75.8 0.3 convolution_bitcast_fusion.1
  76.1 14.9 %all_gather.14 = f32[8,16,64]{0,2,1:T(8,128)S(1)} all-gather(f32[8,16,8]{0,2,1:T(8,128)S(1)} %convolution_bitcast_fusion.1), channel_id=1, replica_groups=mesh['seq'=4,'res'=8] {'res'}, dimensions={2}, use_global_device_ids=true | all-gather | bytes 36864 | tf_op jit(solution)/shard_map/all_gather | solution.py:77
  91.1 0.2 copy.43
  91.2 8.4 %all_gather.15 = f32[8,64,64]{2,0,1:T(8,128)S(1)} all-gather(f32[8,16,64]{2,0,1:T(8,128)S(1)} %copy.43), channel_id=1, replica_groups=mesh['seq'=4,'res'=8] {'seq'}, dimensions={1}, use_global_device_ids=true | all-gather | bytes 163840 | tf_op jit(solution)/shard_map/all_gather | solution.py:78
  99.6 0.1 copy.44
  99.8 0.0 all-to-all-done
  99.8 1.2 bitcast_reduce_fusion
  101.0 0.1 div.42
  101.1 1.3 multiply_reduce_fusion.1
  102.4 0.1 rsqrt.28
  102.5 0.0 copy-done
  102.5 0.0 copy-done.4
  102.5 2.9 %fusion.4 = f32[8,64,1024]{2,1,0:T(8,128)S(1)} fusion(f32[256,1024]{1,0:T(8,128)S(1)} %copy-done, f32[256]{0:T(256)S(1)} %copy-done.4, f32[8,64]{1,0:T(8,128)S(1)} %rsqrt.28, f32[8,64]{1,0:T(8,128)S(1)} %div.42, f32[8,8,8,256]{3,2,1,0:T(8,128)} %all-to-all-done), kind=kOutput, calls=%fused_computation.11 | convolution fusion | flops 1611005952 | bytes 3675136 | tf_op jit(solution)/shard_map/vmap()/dot_general | solution.py:21
  105.5 0.0 copy-done.2
  105.5 1.2 fusion.39
  106.7 2.4 %copy.38 = f32[8,64,256]{1,2,0:T(8,128)} copy(f32[8,64,256]{2,1,0:T(8,128)} %get-tuple-element.2) | data formatting | bytes 1048576 | tf_op jit(solution)/shard_map/vmap()/slice | solution.py:27
  109.1 2.4 %copy.37 = f32[8,64,256]{1,2,0:T(8,128)} copy(f32[8,64,256]{2,1,0:T(8,128)} %get-tuple-element.3) | data formatting | bytes 1048576 | tf_op jit(solution)/shard_map/vmap()/mul | solution.py:24
  111.5 2.4 %copy.36 = f32[8,64,256]{1,2,0:T(8,128)} copy(f32[8,64,256]{2,1,0:T(8,128)} %get-tuple-element.4) | data formatting | bytes 1048576 | tf_op jit(solution)/shard_map/vmap()/slice | solution.py:28
  113.8 5.1 %add_reduce_fusion = (f32[8,8,64]{2,1,0:T(8,128)S(1)}, f32[8,8,64,64]{2,3,1,0:T(8,128)S(1)}) fusion(f32[8,64,64]{1,2,0:T(8,128)S(1)} %copy.44, f32[8,64,8,32]{1,3,2,0:T(8,128)} %bitcast.72, f32[8,64,8,32]{1,3,2,0:T(8,128)} %bitcast.71), kind=kOutput, calls=%fused_computation.4 | convolution fusion | flops 101183488 | bytes 2244608 | tf_op jit(solution)/shard_map/vmap(ihd,jhd->hij)/dot_general | solution.py:30
  118.9 0.0 copy-start.1
  119.0 0.5 fusion.2
  119.5 0.7 copy-done.1
  120.2 3.3 %fusion = f32[8,8,32,64]{3,2,1,0:T(8,128)} fusion(f32[8,64,8,32]{1,3,2,0:T(8,128)S(1)} %bitcast.78, f32[8,8,64,64]{2,3,1,0:T(8,128)S(1)} %get-tuple-element.10, f32[8,8,64]{2,1,0:T(8,128)S(1)} %fusion.2, f32[8,8,64]{2,1,0:T(8,128)S(1)} %get-tuple-element.9, f32[8,64,64]{1,2,0:T(8,128)S(1)} %copy.44), kind=kOutput, calls=%fused_computation | convolution fusion | flops 101449728 | bytes 2260992 | tf_op jit(solution)/shard_map/vmap(hij,jhd->ihd)/dot_general | solution.py:32
  123.5 2.3 %copy.46 = f32[8,64,256]{2,1,0:T(8,128)} copy(f32[8,64,256]{1,2,0:T(8,128)} %bitcast.79) | data formatting | bytes 1048576 | tf_op jit(solution)/shard_map/vmap()/reshape | solution.py:32
  125.8 1.9 %fusion.3 = f32[1,8,64,256]{3,2,1,0:T(8,128)S(1)} fusion(f32[8,64,256]{2,1,0:T(8,128)} %copy.46, f32[8,64,1024]{2,1,0:T(8,128)S(1)} %fusion.4, f32[256,256]{1,0:T(8,128)} %param.19, f32[8,8,8,256]{3,2,1,0:T(8,128)} %all-to-all-done), kind=kOutput, calls=%fused_computation.7 | convolution fusion | flops 403308544 | bytes 2359296 | tf_op jit(solution)/shard_map/vmap()/dot_general | solution.py:36
  127.8 0.3 copy.47
  128.1 19.8 %all_to_all.48 = f32[1,8,64,256]{3,1,0,2:T(8,128)S(1)} all-to-all(f32[1,8,64,256]{3,1,0,2:T(8,128)S(1)} %copy.47), channel_id=1, replica_groups=mesh['seq'=4,'res'=8] {'res'}, dimensions={2} | all-to-all | bytes 1048576 | tf_op jit(solution)/shard_map/all_to_all | solution.py:92
  148.0 1.0 copy.48
  (8 shorter events, 0.1 us)
Async XLA Ops:
  0.6 101.9 %copy-start = (f32[256,1024]{1,0:T(8,128)S(1)}, f32[256,1024]{1,0:T(8,128)}, u32[]{:S(2)}) copy-start(f32[256,1024]{1,0:T(8,128)} %param.18) | copy-start | bytes 3145732
  35.0 22.6 %all-to-all-start.1 = ((f32[4,1,32768]{2,1,0:T(1,128)}), f32[4,1,32768]{2,1,0:T(1,128)S(1)}, u32[]{:S(2)}, u32[]{:S(2)}) async-start(f32[4,1,32768]{2,1,0:T(1,128)} %reshape.99), calls=%async_computation.1 | async-start | bytes 1048576 | tf_op jit(solution)/shard_map/all_to_all | solution.py:64
  57.6 42.2 %all-to-all-start = ((f32[8,8,8,256]{3,2,1,0:T(8,128)}), f32[8,8,8,256]{3,2,1,0:T(8,128)}, u32[]{:S(2)}, u32[]{:S(2)}) async-start(f32[8,8,8,256]{3,2,1,0:T(8,128)} %bitcast), calls=%async_computation | async-start | bytes 1048576 | tf_op jit(solution)/shard_map/all_to_all | solution.py:85
  71.9 1.8 %copy-start.3 = (f32[16,8,128]{2,1,0:T(8,128)S(1)}, f32[16,8,128]{2,1,0:T(8,128)}, u32[]{:S(2)}) copy-start(f32[16,8,128]{2,1,0:T(8,128)} %param.11) | copy-start | bytes 196612
  71.9 3.9 %copy-start.5 = (f32[128,8]{0,1:T(8,128)S(1)}, f32[128,8]{0,1:T(8,128)}, u32[]{:S(2)}) copy-start(f32[128,8]{0,1:T(8,128)} %param.16) | copy-start | bytes 12292
  71.9 3.9 %copy-start.6 = (f32[128]{0:T(128)S(1)}, f32[128]{0:T(128)}, u32[]{:S(2)}) copy-start(f32[128]{0:T(128)} %param.15) | copy-start | bytes 1540
  75.6 29.8 %copy-start.2 = (f32[16,8,128]{2,1,0:T(8,128)}, f32[16,8,128]{2,1,0:T(8,128)S(1)}, u32[]{:S(2)}) copy-start(f32[16,8,128]{2,1,0:T(8,128)S(1)} %get-tuple-element.8) | copy-start | bytes 196612
  75.6 26.9 %copy-start.4 = (f32[256]{0:T(256)S(1)}, f32[256]{0:T(256)}, u32[]{:S(2)}) copy-start(f32[256]{0:T(256)} %param.17) | copy-start | bytes 3076
  118.9 1.2 copy-start.1
where the time goes:
time: 150 us; the launch traced here: 149 us
  blocking collectives  86.8 us (58%)
  local copies, waits for them, and re-layouts  23.6 us (16%)
  matrix products  20.3 us (14%)
  other arithmetic  9.14 us (6%)
  starting transfers between devices  8.05 us (5%)
    all_gather x1, blocking collectives, on_device(): left_all = lax.all_gather(left_maps, 'res', axis=2, tiled=True)  25.1 us
    all_to_all x1, blocking collectives, on_device(): lax.all_to_all(attended, 'res', split_axis=2, concat_axis=0, tiled=True)  19.8 us
    all_gather x1, blocking collectives, on_device(): lax.all_gather(right_maps, 'seq', axis=0, tiled=True)  18.5 us
    all_gather x1, blocking collectives, on_device(): bias_rows = lax.all_gather(bias_tile, 'res', axis=2, tiled=True)  14.9 us
    all_gather x1, blocking collectives, on_device(): bias_all = lax.all_gather(bias_rows, 'seq', axis=1, tiled=True)  8.4 us
    dot_general x1, matrix products, row_attention(): jnp.einsum('ihd,jhd->hij', query_map, key_map, precision=precise) + bias_all  5.09 us
    all_to_all x1, starting transfers between devices, on_device(): lax.all_to_all(sequence_grouped_rows, 'res', split_axis=0, concat_axis=2,...  4.34 us
    div x2, local copies, waits for them, and re-layouts, on_device(): summed / seq_total  4 us
  transfers between devices with their start and end apart: 2, of which 0 were waited for; matrix products, arithmetic and copies ran while one was open for 10% of the time, Pallas kernels for 0%

commit v1 on v0

--- a/solution.py
+++ b/solution.py
@@ -74,7 +74,12 @@
     bias_tile = jnp.einsum(
         "ijc,ch->hij", layer_norm(updated_pair_array, pair_gain), w_bias, precision=precise
     )
-    bias_rows = lax.all_gather(bias_tile, "res", axis=2, tiled=True)
+    ring = [bias_tile]
+    for hop in range(7):
+        ring.append(lax.ppermute(ring[-1], "res", [(dev, (dev + 1) % 8) for dev in range(8)]))
+    bias_rows = jnp.roll(
+        jnp.concatenate(ring[::-1], axis=2), (lax.axis_index("res") + 1) * ring[0].shape[2], axis=2
+    )
     bias_all = lax.all_gather(bias_rows, "seq", axis=1, tiled=True)
     sequence_grouped_rows = alignment.reshape(
         sequence_group_list,

time: 150 us -> 172 us (1.15)
  waiting for transfers between devices: 0.01 us -> 38.2 us
  blocking collectives: 86.8 us -> 69.8 us
    ppermute x0 -> x7, waiting for transfers between devices: none -> 38.2 us  [on_device(): lax.ppermute(ring[-1], 'res', [(dev, (dev + 1) % 8) for dev in range(8)])]
    all_gather x1 -> x0, blocking collectives: 14.9 us -> none  [on_device(): bias_rows = lax.all_gather(bias_tile, 'res', axis=2, tiled=True)]
    all_to_all x1, blocking collectives: 19.8 us -> 17.7 us  [on_device(): lax.all_to_all(attended, 'res', split_axis=2, concat_axis=0, tiled=True)]
  transfers between devices with their start and end apart: 2 -> 9, of which waited for: 0 -> 7; matrix products, arithmetic and copies ran while one was open for 10% -> 9% of each run, Pallas kernels for 0% -> 0%
where the time goes in v1:
time: 172 us; the launch traced here: 171 us
  blocking collectives  69.8 us (41%)
  waiting for transfers between devices  38.2 us (22%)
  local copies, waits for them, and re-layouts  23.9 us (14%)
  matrix products  21.1 us (12%)
  other arithmetic  9.14 us (5%)
  starting transfers between devices  8.29 us (5%)
    ppermute x7, waiting for transfers between devices, on_device(): lax.ppermute(ring[-1], 'res', [(dev, (dev + 1) % 8) for dev in range(8)])  38.2 us
    all_gather x1, blocking collectives, on_device(): left_all = lax.all_gather(left_maps, 'res', axis=2, tiled=True)  25.1 us
    all_gather x1, blocking collectives, on_device(): lax.all_gather(right_maps, 'seq', axis=0, tiled=True)  18.5 us
    all_to_all x1, blocking collectives, on_device(): lax.all_to_all(attended, 'res', split_axis=2, concat_axis=0, tiled=True)  17.7 us
    all_gather x1, blocking collectives, on_device(): bias_all = lax.all_gather(bias_rows, 'seq', axis=1, tiled=True)  8.39 us
    dot_general x1, matrix products, row_attention(): jnp.einsum('ihd,jhd->hij', query_map, key_map, precision=precise) + bias_all  5.09 us
    all_to_all x1, starting transfers between devices, on_device(): lax.all_to_all(sequence_grouped_rows, 'res', split_axis=0, concat_axis=2,...  4.34 us
    div x2, local copies, waits for them, and re-layouts, on_device(): summed / seq_total  4 us
  transfers between devices with their start and end apart: 9, of which 7 were waited for; matrix products, arithmetic and copies ran while one was open for 9% of the time, Pallas kernels for 0%

profile of v1, /device:TPU:0, one launch (start us, length us, event | category | flops | bytes accessed | tf_op | source)
XLA Modules:
  0.0 171.3 jit_solution(6462826501815504274)
XLA Ops:
  0.6 0.0 copy-start
  0.6 1.3 reduce_sum.65
  1.9 1.3 multiply_reduce_fusion
  3.2 1.7 convolution_bitcast_fusion
  4.9 0.1 fusion.40
  5.1 25.1 %all_gather.10 = f32[64,32,64]{1,2,0:T(8,128)S(1)} all-gather(f32[64,32,8]{1,2,0:T(8,128)S(1)} %get-tuple-element.5), channel_id=1, replica_groups=mesh['seq'=4,'res'=8] {'res'}, dimensions={2}, use_global_device_ids=true | all-gather | bytes 589824 | tf_op jit(solution)/shard_map/all_gather | solution.py:63
  30.2 2.1 %copy.39 = f32[64,32,64]{0,1,2:T(8,128)} copy(f32[64,32,64]{1,2,0:T(8,128)S(1)} %all_gather.10) | data formatting | bytes 1048576 | tf_op jit(solution)/shard_map/all_gather | solution.py:63
  32.3 2.7 %reshape.99 = f32[4,1,32768]{2,1,0:T(1,128)} reshape(f32[64,32,64]{2,1,0:T(8,128)} %bitcast.73) | data formatting | bytes 1048576
  35.0 3.7 %all-to-all-start.1 = ((f32[4,1,32768]{2,1,0:T(1,128)}), f32[4,1,32768]{2,1,0:T(1,128)S(1)}, u32[]{:S(2)}, u32[]{:S(2)}) async-start(f32[4,1,32768]{2,1,0:T(1,128)} %reshape.99), calls=%async_computation.1 | async-start | bytes 1048576 | tf_op jit(solution)/shard_map/all_to_all | solution.py:64
  38.7 18.5 %all_gather.9 = f32[256,32,8]{1,2,0:T(8,128)S(1)} all-gather(f32[64,32,8]{1,2,0:T(8,128)S(1)} %get-tuple-element.6), channel_id=1, replica_groups=mesh['seq'=4,'res'=8] {'seq'}, dimensions={0}, use_global_device_ids=true | all-gather | bytes 327680 | tf_op jit(solution)/shard_map/all_gather | solution.py:68
  57.2 0.4 copy.48
  57.6 0.0 all-to-all-done.1
  57.6 4.3 %all-to-all-start = ((f32[8,8,8,256]{3,2,1,0:T(8,128)}), f32[8,8,8,256]{3,2,1,0:T(8,128)}, u32[]{:S(2)}, u32[]{:S(2)}) async-start(f32[8,8,8,256]{3,2,1,0:T(8,128)} %bitcast), calls=%async_computation | async-start | bytes 1048576 | tf_op jit(solution)/shard_map/all_to_all | solution.py:90
  62.0 0.5 broadcast.98
  62.5 2.1 %reduce.2 = f32[4,32768]{1,0:T(4,128)S(1)} reduce(f32[4,1,32768]{2,1,0:T(1,128)S(1)} %all-to-all-done.1, f32[]{:T(128)} %broadcast.98), dimensions={1}, to_apply=%all_to_all.38.reduce_sub_computation | reduce | bytes 1048580 | tf_op jit(solution)/shard_map/all_to_all | solution.py:64
  64.6 0.5 reshape.100
  65.2 0.7 copy.58
  65.9 0.6 reshape.94
  66.5 3.2 %multiply_bitcast_fusion = f32[16,8,32,32]{2,1,0,3:T(8,128)} fusion(f32[256,32,8,1]{0,2,3,1:T(8,128)S(1)} %copy.48, f32[256,32,16,1]{0,1,2,3:T(8,128)S(1)} %reshape.94), kind=kOutput, calls=%fused_computation.3 | convolution fusion | flops 402784256 | bytes 1310720 | tf_op jit(solution)/shard_map/sxi,syj->ijxy/dot_general | solution.py:65
  69.7 2.3 %copy.42 = f32[16,8,32,32]{3,2,1,0:T(8,128)S(1)} copy(f32[16,8,32,32]{2,1,0,3:T(8,128)} %multiply_bitcast_fusion) | data formatting | bytes 1048576 | tf_op jit(solution)/shard_map/div | solution.py:72
  71.9 0.0 copy-start.3
  71.9 0.0 copy-start.5
  71.9 0.0 copy-start.6
  72.0 1.7 %div.50 = f32[16,8,1024]{2,1,0:T(8,128)} reshape(f32[16,8,32,32]{3,2,1,0:T(8,128)S(1)} %copy.42) | data formatting | bytes 1048576 | tf_op jit(solution)/shard_map/div | solution.py:72
  73.7 1.9 %fusion.41 = (f32[16,8]{1,0:T(8,128)S(1)}, f32[16,8,128]{2,1,0:T(8,128)S(1)}) fusion(f32[16,8,128]{2,1,0:T(8,128)S(1)} %copy-done.3, f32[16,8,1024]{2,1,0:T(8,128)} %div.50, f32[1024,128]{1,0:T(8,128)} %param.14), kind=kOutput, calls=%fused_computation.61 | convolution fusion | flops 201359232 | bytes 1180160 | tf_op jit(solution)/shard_map/ijk,kc->ijc/dot_general | solution.py:72
  75.6 0.0 copy-start.2
  75.6 0.0 copy-start.4
  75.7 0.2 multiply_reduce_fusion.2
  75.8 1.0 convolution_bitcast_fusion.1
  76.9 0.2 collective-permute-start
  77.1 5.3 %collective-permute-done = f32[8,16,8]{2,0,1:T(8,128)S(1)} collective-permute-done((f32[8,16,8]{2,0,1:T(8,128)S(1)}, f32[8,16,8]{2,0,1:T(8,128)S(1)}, u32[]{:S(2)}, u32[]{:S(2)}) %collective-permute-start) | collective-permute-done | bytes 4128 | tf_op jit(solution)/shard_map/ppermute | solution.py:79
  82.4 0.0 collective-permute-start.1
  82.4 5.5 %collective-permute-done.1 = f32[8,16,8]{2,0,1:T(8,128)S(1)} collective-permute-done((f32[8,16,8]{2,0,1:T(8,128)S(1)}, f32[8,16,8]{2,0,1:T(8,128)S(1)}, u32[]{:S(2)}, u32[]{:S(2)}) %collective-permute-start.1) | collective-permute-done | bytes 4128 | tf_op jit(solution)/shard_map/ppermute | solution.py:79
  87.9 0.0 collective-permute-start.2
  87.9 5.5 %collective-permute-done.2 = f32[8,16,8]{2,0,1:T(8,128)S(1)} collective-permute-done((f32[8,16,8]{2,0,1:T(8,128)S(1)}, f32[8,16,8]{2,0,1:T(8,128)S(1)}, u32[]{:S(2)}, u32[]{:S(2)}) %collective-permute-start.2) | collective-permute-done | bytes 4128 | tf_op jit(solution)/shard_map/ppermute | solution.py:79
  93.4 0.0 collective-permute-start.3
  93.4 5.5 %collective-permute-done.3 = f32[8,16,8]{2,0,1:T(8,128)S(1)} collective-permute-done((f32[8,16,8]{2,0,1:T(8,128)S(1)}, f32[8,16,8]{2,0,1:T(8,128)S(1)}, u32[]{:S(2)}, u32[]{:S(2)}) %collective-permute-start.3) | collective-permute-done | bytes 4128 | tf_op jit(solution)/shard_map/ppermute | solution.py:79
  98.9 5.5 %collective-permute-done.4 = f32[8,16,8]{2,0,1:T(8,128)S(1)} collective-permute-done((f32[8,16,8]{2,0,1:T(8,128)S(1)}, f32[8,16,8]{2,0,1:T(8,128)S(1)}, u32[]{:S(2)}, u32[]{:S(2)}) %collective-permute-start.4) | collective-permute-done | bytes 4128 | tf_op jit(solution)/shard_map/ppermute | solution.py:79
  104.4 0.0 collective-permute-start.5
  104.4 5.5 %collective-permute-done.5 = f32[8,16,8]{2,0,1:T(8,128)S(1)} collective-permute-done((f32[8,16,8]{2,0,1:T(8,128)S(1)}, f32[8,16,8]{2,0,1:T(8,128)S(1)}, u32[]{:S(2)}, u32[]{:S(2)}) %collective-permute-start.5) | collective-permute-done | bytes 4128 | tf_op jit(solution)/shard_map/ppermute | solution.py:79
  109.9 0.0 collective-permute-start.6
  109.9 5.5 %collective-permute-done.6 = f32[8,16,8]{2,0,1:T(8,128)S(1)} collective-permute-done((f32[8,16,8]{2,0,1:T(8,128)S(1)}, f32[8,16,8]{2,0,1:T(8,128)S(1)}, u32[]{:S(2)}, u32[]{:S(2)}) %collective-permute-start.6) | collective-permute-done | bytes 4128 | tf_op jit(solution)/shard_map/ppermute | solution.py:79
  115.3 0.3 concatenate.6
  115.7 0.1 constant_dynamic-slice_fusion
  115.8 8.4 %all_gather.11 = f32[8,64,64]{2,0,1:T(8,128)S(1)} all-gather(f32[8,16,64]{2,0,1:T(8,128)S(1)} %constant_dynamic-slice_fusion), channel_id=1, replica_groups=mesh['seq'=4,'res'=8] {'seq'}, dimensions={1}, use_global_device_ids=true | all-gather | bytes 163840 | tf_op jit(solution)/shard_map/all_gather | solution.py:83
  124.2 0.1 copy.43
  124.3 1.2 bitcast_reduce_fusion
  125.5 0.1 div.42
  125.6 1.3 multiply_reduce_fusion.1
  127.0 0.1 rsqrt.28
  127.0 2.9 %fusion.4 = f32[8,64,1024]{2,1,0:T(8,128)S(1)} fusion(f32[256,1024]{1,0:T(8,128)S(1)} %copy-done, f32[256]{0:T(256)S(1)} %copy-done.4, f32[8,64]{1,0:T(8,128)S(1)} %rsqrt.28, f32[8,64]{1,0:T(8,128)S(1)} %div.42, f32[8,8,8,256]{3,2,1,0:T(8,128)} %all-to-all-done), kind=kOutput, calls=%fused_computation.11 | convolution fusion | flops 1611005952 | bytes 3675136 | tf_op jit(solution)/shard_map/vmap()/dot_general | solution.py:21
  130.0 1.2 fusion.39
  131.2 2.4 %copy.38 = f32[8,64,256]{1,2,0:T(8,128)} copy(f32[8,64,256]{2,1,0:T(8,128)} %get-tuple-element.2) | data formatting | bytes 1048576 | tf_op jit(solution)/shard_map/vmap()/slice | solution.py:27
  133.6 2.4 %copy.37 = f32[8,64,256]{1,2,0:T(8,128)} copy(f32[8,64,256]{2,1,0:T(8,128)} %get-tuple-element.3) | data formatting | bytes 1048576 | tf_op jit(solution)/shard_map/vmap()/mul | solution.py:24
  136.0 2.4 %copy.36 = f32[8,64,256]{1,2,0:T(8,128)} copy(f32[8,64,256]{2,1,0:T(8,128)} %get-tuple-element.4) | data formatting | bytes 1048576 | tf_op jit(solution)/shard_map/vmap()/slice | solution.py:28
  138.4 5.1 %add_reduce_fusion = (f32[8,8,64]{2,1,0:T(8,128)S(1)}, f32[8,8,64,64]{2,3,1,0:T(8,128)S(1)}) fusion(f32[8,64,64]{1,2,0:T(8,128)S(1)} %copy.43, f32[8,64,8,32]{1,3,2,0:T(8,128)} %bitcast.72, f32[8,64,8,32]{1,3,2,0:T(8,128)} %bitcast.71), kind=kOutput, calls=%fused_computation.4 | convolution fusion | flops 101183488 | bytes 2244608 | tf_op jit(solution)/shard_map/vmap(ihd,jhd->hij)/dot_general | solution.py:30
  143.5 0.5 fusion.2
  144.0 0.7 copy-done.1
  144.7 3.3 %fusion = f32[8,8,32,64]{3,2,1,0:T(8,128)} fusion(f32[8,64,8,32]{1,3,2,0:T(8,128)S(1)} %bitcast.78, f32[8,8,64,64]{2,3,1,0:T(8,128)S(1)} %get-tuple-element.10, f32[8,8,64]{2,1,0:T(8,128)S(1)} %fusion.2, f32[8,8,64]{2,1,0:T(8,128)S(1)} %get-tuple-element.9, f32[8,64,64]{1,2,0:T(8,128)S(1)} %copy.43), kind=kOutput, calls=%fused_computation | convolution fusion | flops 101449728 | bytes 2260992 | tf_op jit(solution)/shard_map/vmap(hij,jhd->ihd)/dot_general | solution.py:32
  148.0 2.3 %copy.45 = f32[8,64,256]{2,1,0:T(8,128)} copy(f32[8,64,256]{1,2,0:T(8,128)} %bitcast.79) | data formatting | bytes 1048576 | tf_op jit(solution)/shard_map/vmap()/reshape | solution.py:32
  150.4 2.0 %fusion.3 = f32[1,8,64,256]{3,2,1,0:T(8,128)S(1)} fusion(f32[8,64,256]{2,1,0:T(8,128)} %copy.45, f32[8,64,1024]{2,1,0:T(8,128)S(1)} %fusion.4, f32[256,256]{1,0:T(8,128)} %param.19, f32[8,8,8,256]{3,2,1,0:T(8,128)} %all-to-all-done), kind=kOutput, calls=%fused_computation.7 | convolution fusion | flops 403308544 | bytes 2359296 | tf_op jit(solution)/shard_map/vmap()/dot_general | solution.py:36
  152.3 0.3 copy.46
  152.6 17.7 %all_to_all.48 = f32[1,8,64,256]{3,1,0,2:T(8,128)S(1)} all-to-all(f32[1,8,64,256]{3,1,0,2:T(8,128)S(1)} %copy.46), channel_id=1, replica_groups=mesh['seq'=4,'res'=8] {'res'}, dimensions={2} | all-to-all | bytes 1048576 | tf_op jit(solution)/shard_map/all_to_all | solution.py:97
  170.4 1.0 copy.47
  (17 shorter events, 0.1 us)
Async XLA Ops:
  0.6 126.4 %copy-start = (f32[256,1024]{1,0:T(8,128)S(1)}, f32[256,1024]{1,0:T(8,128)}, u32[]{:S(2)}) copy-start(f32[256,1024]{1,0:T(8,128)} %param.18) | copy-start | bytes 3145732
  35.0 22.6 %all-to-all-start.1 = ((f32[4,1,32768]{2,1,0:T(1,128)}), f32[4,1,32768]{2,1,0:T(1,128)S(1)}, u32[]{:S(2)}, u32[]{:S(2)}) async-start(f32[4,1,32768]{2,1,0:T(1,128)} %reshape.99), calls=%async_computation.1 | async-start | bytes 1048576 | tf_op jit(solution)/shard_map/all_to_all | solution.py:64
  57.6 66.7 %all-to-all-start = ((f32[8,8,8,256]{3,2,1,0:T(8,128)}), f32[8,8,8,256]{3,2,1,0:T(8,128)}, u32[]{:S(2)}, u32[]{:S(2)}) async-start(f32[8,8,8,256]{3,2,1,0:T(8,128)} %bitcast), calls=%async_computation | async-start | bytes 1048576 | tf_op jit(solution)/shard_map/all_to_all | solution.py:90
  71.9 1.8 %copy-start.3 = (f32[16,8,128]{2,1,0:T(8,128)S(1)}, f32[16,8,128]{2,1,0:T(8,128)}, u32[]{:S(2)}) copy-start(f32[16,8,128]{2,1,0:T(8,128)} %param.11) | copy-start | bytes 196612
  71.9 3.9 %copy-start.5 = (f32[128,8]{0,1:T(8,128)S(1)}, f32[128,8]{0,1:T(8,128)}, u32[]{:S(2)}) copy-start(f32[128,8]{0,1:T(8,128)} %param.16) | copy-start | bytes 12292
  71.9 3.9 %copy-start.6 = (f32[128]{0:T(128)S(1)}, f32[128]{0:T(128)}, u32[]{:S(2)}) copy-start(f32[128]{0:T(128)} %param.15) | copy-start | bytes 1540
  75.6 54.4 %copy-start.2 = (f32[16,8,128]{2,1,0:T(8,128)}, f32[16,8,128]{2,1,0:T(8,128)S(1)}, u32[]{:S(2)}) copy-start(f32[16,8,128]{2,1,0:T(8,128)S(1)} %get-tuple-element.8) | copy-start | bytes 196612
  75.6 51.4 %copy-start.4 = (f32[256]{0:T(256)S(1)}, f32[256]{0:T(256)}, u32[]{:S(2)}) copy-start(f32[256]{0:T(256)} %param.17) | copy-start | bytes 3076
  76.9 5.5 %collective-permute-start = (f32[8,16,8]{2,0,1:T(8,128)S(1)}, f32[8,16,8]{2,0,1:T(8,128)S(1)}, u32[]{:S(2)}, u32[]{:S(2)}) collective-permute-start(f32[8,16,8]{2,0,1:T(8,128)S(1)} %convolution_bitcast_fusion.1), channel_id=1, source_target_pairs={{0,1},{1,2},{2,3},{3,4},{4,5},{5,6},{6,7},{7,0},{8,9},{9,10},{10,1... | collective-permute-start | bytes 12296 | tf_op jit(solution)/shard_map/ppermute | solution.py:79
  82.4 5.5 %collective-permute-start.1 = (f32[8,16,8]{2,0,1:T(8,128)S(1)}, f32[8,16,8]{2,0,1:T(8,128)S(1)}, u32[]{:S(2)}, u32[]{:S(2)}) collective-permute-start(f32[8,16,8]{2,0,1:T(8,128)S(1)} %collective-permute-done), channel_id=1, source_target_pairs={{0,1},{1,2},{2,3},{3,4},{4,5},{5,6},{6,7},{7,0},{8,9},{9,10},{10,1... | collective-permute-start | bytes 12296 | tf_op jit(solution)/shard_map/ppermute | solution.py:79
  87.9 5.5 %collective-permute-start.2 = (f32[8,16,8]{2,0,1:T(8,128)S(1)}, f32[8,16,8]{2,0,1:T(8,128)S(1)}, u32[]{:S(2)}, u32[]{:S(2)}) collective-permute-start(f32[8,16,8]{2,0,1:T(8,128)S(1)} %collective-permute-done.1), channel_id=1, source_target_pairs={{0,1},{1,2},{2,3},{3,4},{4,5},{5,6},{6,7},{7,0},{8,9},{9,10},{10,1... | collective-permute-start | bytes 12296 | tf_op jit(solution)/shard_map/ppermute | solution.py:79
  93.4 5.5 %collective-permute-start.3 = (f32[8,16,8]{2,0,1:T(8,128)S(1)}, f32[8,16,8]{2,0,1:T(8,128)S(1)}, u32[]{:S(2)}, u32[]{:S(2)}) collective-permute-start(f32[8,16,8]{2,0,1:T(8,128)S(1)} %collective-permute-done.2), channel_id=1, source_target_pairs={{0,1},{1,2},{2,3},{3,4},{4,5},{5,6},{6,7},{7,0},{8,9},{9,10},{10,1... | collective-permute-start | bytes 12296 | tf_op jit(solution)/shard_map/ppermute | solution.py:79
  98.9 5.5 %collective-permute-start.4 = (f32[8,16,8]{2,0,1:T(8,128)S(1)}, f32[8,16,8]{2,0,1:T(8,128)S(1)}, u32[]{:S(2)}, u32[]{:S(2)}) collective-permute-start(f32[8,16,8]{2,0,1:T(8,128)S(1)} %collective-permute-done.3), channel_id=1, source_target_pairs={{0,1},{1,2},{2,3},{3,4},{4,5},{5,6},{6,7},{7,0},{8,9},{9,10},{10,1... | collective-permute-start | bytes 12296 | tf_op jit(solution)/shard_map/ppermute | solution.py:79
  104.4 5.5 %collective-permute-start.5 = (f32[8,16,8]{2,0,1:T(8,128)S(1)}, f32[8,16,8]{2,0,1:T(8,128)S(1)}, u32[]{:S(2)}, u32[]{:S(2)}) collective-permute-start(f32[8,16,8]{2,0,1:T(8,128)S(1)} %collective-permute-done.4), channel_id=1, source_target_pairs={{0,1},{1,2},{2,3},{3,4},{4,5},{5,6},{6,7},{7,0},{8,9},{9,10},{10,1... | collective-permute-start | bytes 12296 | tf_op jit(solution)/shard_map/ppermute | solution.py:79
  109.9 5.5 %collective-permute-start.6 = (f32[8,16,8]{2,0,1:T(8,128)S(1)}, f32[8,16,8]{2,0,1:T(8,128)S(1)}, u32[]{:S(2)}, u32[]{:S(2)}) collective-permute-start(f32[8,16,8]{2,0,1:T(8,128)S(1)} %collective-permute-done.5), channel_id=1, source_target_pairs={{0,1},{1,2},{2,3},{3,4},{4,5},{5,6},{6,7},{7,0},{8,9},{9,10},{10,1... | collective-permute-start | bytes 12296 | tf_op jit(solution)/shard_map/ppermute | solution.py:79
  143.5 1.2 copy-start.1
